TPU v7x, 256 devices: a whole 4x4x8 slice. The times are simulated.
256 devices in a mesh: row: 64 (over z, y, core), col: 4 (over x).
Axes of the slice: x: 4, y: 4, z: 8, core: 2. Of those that a mesh axis runs over, the one named last changes fastest.
Arguments:
- sigma_anc: float32 [8192, 8192], P('row', 'col'), may hold values from -24 to 80, as said below
- panel_hat: float32 [8192, 4096], P('row', 'col'), may hold values from -0.0625 to 0.0625
- pattern: int32 [64, 64], replicated, may hold values from 0 to 1, as said below
- diag_inverse: float32 [4096], P('col'), may hold values from 0.5 to 4
Outputs:
- sigma_cross: float32 [8192, 4096], P('row', 'col')
- variance: float32 [4096], P('col')
Inputs may be any that keep to these rules, and one draw needn't show every extreme that they name: `pattern`: symmetric; every diagonal block is 1. `sigma_anc`: symmetric.
All inputs are finite; a program needn't handle non-finite values.
Results may differ from a plain program's by a relative error of at most 0.000073.
Values sent between devices are 32-bit elements; how exact they have to be, the bound alone decides.
A program may use at most 128 MiB of HBM per device.

v0:
```python
import jax
import jax.numpy as jnp
from jax import lax
from jax.sharding import PartitionSpec as P


def body(sigma_anc, panel_hat, pattern, diag_inverse):
    sigma_rows = lax.all_gather(sigma_anc, "col", axis=1, tiled=True)
    band_rows = sigma_rows.shape[0]
    ancestors = sigma_rows.shape[1]
    blocks = pattern.shape[0]
    block_width = ancestors // blocks
    row_start = lax.axis_index("row") * band_rows
    global_rows = row_start + lax.iota(jnp.int32, band_rows)
    row_onehot = (
        global_rows[:, None] // block_width == lax.iota(jnp.int32, blocks)[None, :]
    ).astype(jnp.float32)
    row_mask = jnp.dot(row_onehot, pattern.astype(jnp.float32), preferred_element_type=jnp.float32)
    expanded = jnp.broadcast_to(row_mask[:, :, None], (band_rows, blocks, block_width)).reshape(
        band_rows, ancestors
    )
    masked = sigma_rows * expanded
    product = jnp.dot(
        masked,
        lax.all_gather(panel_hat, "row", axis=0, tiled=True),
        precision=lax.Precision.HIGHEST,
        preferred_element_type=jnp.float32,
    )
    sigma_cross = -product
    partial_value = jnp.sum(panel_hat * sigma_cross, axis=0)
    summed = lax.psum(partial_value, "row")
    variance = diag_inverse - summed
    return (sigma_cross, variance)


def solution(mesh):
    in_specs = (P("row", "col"), P("row", "col"), P(), P("col"))
    out_specs = (P("row", "col"), P("col"))
    return jax.shard_map(body, mesh=mesh, in_specs=in_specs, out_specs=out_specs, check_vma=False)
```

profile of v0, /device:TPU:2, one launch (start us, length us, event | category | flops | bytes accessed | tf_op | source)
XLA Modules:
  0.0 369.2 jit_solution(3616185705939488497)
XLA Ops:
  7.2 0.0 copy-start.1
  7.2 0.0 all-gather.3.cloned.1.call-start
  7.2 0.7 all-gather.3.cloned.1.call-update
  7.9 0.0 all-gather.5.cloned.1.call-start
  8.0 0.7 all-gather.5.cloned.1.call-update
  8.7 1.0 fusion.3
  9.6 53.2 %all-gather.3.cloned.1.call-done = f32[128,8192]{1,0:T(8,128)} async-done(((f32[128,2048]{1,0:T(8,128)}), f32[128,8192]{1,0:T(8,128)}) %all-gather.3.cloned.1.call-update) | async-done | bytes 4194320 | tf_op jit(solution)/shard_map/all_gather | solution.py:8
  62.9 145.4 %all-gather.5.cloned.1.call-done = f32[8192,1024]{1,0:T(8,128)} async-done(((f32[128,1024]{1,0:T(8,128)}), f32[8192,1024]{1,0:T(8,128)}) %all-gather.5.cloned.1.call-update) | async-done | bytes 33554448 | tf_op jit(solution)/shard_map/all_gather | solution.py:25
  208.3 0.0 copy-start
  208.3 1.1 broadcast_in_dim.2
  209.4 0.0 copy-done.1
  209.5 1.0 copy-done
  210.5 0.0 copy-start.2
  210.5 25.7 %multiply_reduce_fusion = (f32[1024]{0:T(1024)S(1)}, f32[128,1024]{1,0:T(8,128)}) fusion(f32[128,1024]{1,0:T(8,128)S(1)} %copy-done.1, f32[8192,1024]{1,0:T(8,128)} %all-gather.5.cloned.1.call-done, f32[128,8192]{1,0:T(8,128)S(1)} %copy-done, f32[16,8,64,128]{3,2,1,0:T(8,128)S(1)} %bitcast.9), kind=kOutput, calls=%fused_computation.4 | convolution fusion | flops 12886342656 | bytes 42995712 | tf_op jit(solution)/shard_map/dot_general | solution.py:23
  236.2 125.5 %psum.7 = f32[1024]{0:T(1024)S(1)} all-reduce(f32[1024]{0:T(1024)S(1)} %get-tuple-element.2), channel_id=1, replica_groups=mesh['row'=64,'col'=4] {'row'}, use_global_device_ids=true, to_apply=%region_1.2 | all-reduce | flops 1024 | bytes 8192 | tf_op jit(solution)/shard_map/psum | solution.py:31
  361.7 0.0 copy-done.2
  361.7 0.6 sub.10
  (1 shorter events, 0.0 us)
Async XLA Ops:
  7.2 202.3 %copy-start.1 = (f32[128,1024]{1,0:T(8,128)S(1)}, f32[128,1024]{1,0:T(8,128)}, u32[]{:S(2)}) copy-start(f32[128,1024]{1,0:T(8,128)} %param.5) | copy-start | bytes 1572868
  7.2 55.7 %all-gather.3.cloned.1.call-start = ((), (), s32[]{:S(2)}) async-start(), calls=%async_computation | async-start | bytes 5242880 | tf_op jit(solution)/shard_map/all_gather | solution.py:8
  7.9 200.4 %all-gather.5.cloned.1.call-start = ((), (), s32[]{:S(2)}) async-start(), calls=%async_computation.1 | async-start | bytes 34078720 | tf_op jit(solution)/shard_map/all_gather | solution.py:25
  208.3 2.2 copy-start
  210.5 151.2 %copy-start.2 = (f32[1024]{0:T(1024)S(1)}, f32[1024]{0:T(1024)}, u32[]{:S(2)}) copy-start(f32[1024]{0:T(1024)} %param.7) | copy-start | bytes 12292
Sparse Core Ops, SparseCore 0:
  9.8 53.0 all-gather.2
  65.6 142.6 all-gather.4
where the time goes:
time: 369 us
  waiting for transfers between devices  200 us (54%)
  blocking collectives  126 us (34%)
  matrix products  26.7 us (7%)
  between operations  14.1 us (4%)
    all_gather x1, waiting for transfers between devices, body(): lax.all_gather(panel_hat, 'row', axis=0, tiled=True)  145 us
    psum x1, blocking collectives, body(): summed = lax.psum(partial_value, 'row')  126 us
    all_gather x1, waiting for transfers between devices, body(): sigma_rows = lax.all_gather(sigma_anc, 'col', axis=1, tiled=True)  53.2 us
    dot_general x1, matrix products, body(): jnp.dot(masked, lax.all_gather(panel_hat, 'row', axis=0, tiled=True), pre...  25.7 us
  transfers between devices with their start and end apart: 2, of which 2 were waited for; matrix products, arithmetic and copies ran while one was open for 0% of the time, Pallas kernels for 0%

commit v1 on v0

--- a/solution.py
+++ b/solution.py
@@ -22,7 +22,9 @@
     masked = sigma_rows * expanded
     product = jnp.dot(
         masked,
-        lax.all_gather(panel_hat, "row", axis=0, tiled=True),
+        jnp.concatenate(
+            lax.all_to_all(jnp.stack(lax.psum(1, "row") * [panel_hat]), "row", 0, 0), axis=0
+        ),
         precision=lax.Precision.HIGHEST,
         preferred_element_type=jnp.float32,
     )

time: 369 us -> 933 us (2.53)
  waiting for transfers between devices: 200 us -> 730 us
  starting transfers between devices: 0.08 us -> 12.5 us
  local copies, waits for them, and re-layouts: 2.19 us -> 14.3 us
    all_to_all x0 -> x1, waiting for transfers between devices: none -> 676 us  [body(): lax.all_to_all(jnp.stack(lax.psum(1, 'row') * [panel_hat]), 'row', 0, 0)]
    all_gather x1 -> x0, waiting for transfers between devices: 145 us -> none  [body(): lax.all_gather(panel_hat, 'row', axis=0, tiled=True)]
    all_to_all x0 -> x1, starting transfers between devices: none -> 12.5 us  [body(): lax.all_to_all(jnp.stack(lax.psum(1, 'row') * [panel_hat]), 'row', 0, 0)]
    another operation x0 -> x1, local copies, waits for them, and re-layouts: none -> 12.1 us  [body(): jnp.stack(lax.psum(1, 'row') * [panel_hat])]
    psum x1, blocking collectives: 126 us -> 135 us  [body(): summed = lax.psum(partial_value, 'row')]
where the time goes in v1:
time: 933 us; the launch traced here: 932 us
  waiting for transfers between devices  730 us (78%)
  blocking collectives  135 us (14%)
  matrix products  25.9 us (3%)
  local copies, waits for them, and re-layouts  14.3 us (2%)
  between operations  14.1 us (2%)
  starting transfers between devices  12.5 us (1%)
    all_to_all x1, waiting for transfers between devices, body(): lax.all_to_all(jnp.stack(lax.psum(1, 'row') * [panel_hat]), 'row', 0, 0)  676 us
    psum x1, blocking collectives, body(): summed = lax.psum(partial_value, 'row')  135 us
    all_gather x1, waiting for transfers between devices, body(): sigma_rows = lax.all_gather(sigma_anc, 'col', axis=1, tiled=True)  52.9 us
    dot_general x1, matrix products, body(): jnp.dot(masked, jnp.concatenate(lax.all_to_all(jnp.stack(lax.psum(1, 'row...  25.7 us
  transfers between devices with their start and end apart: 2, of which 2 were waited for; matrix products, arithmetic and copies ran while one was open for 0% of the time, Pallas kernels for 0%

profile of v1, /device:TPU:2, one launch (start us, length us, event | category | flops | bytes accessed | tf_op | source)
XLA Modules:
  0.0 932.4 jit_solution(8684928712854991326)
XLA Ops:
  7.2 12.1 %stack.2 = f32[64,128,1024]{2,1,0:T(8,128)} broadcast(f32[128,1024]{1,0:T(8,128)} %param.5), dimensions={1,2} | broadcast | bytes 34078720 | tf_op jit(solution)/shard_map/stack | solution.py:26
  19.2 0.0 copy-start.2
  19.3 12.5 %all-to-all-start = ((f32[64,128,1024]{2,1,0:T(8,128)}), f32[64,128,1024]{2,1,0:T(8,128)}, u32[]{:S(2)}, u32[]{:S(2)}) async-start(f32[64,128,1024]{2,1,0:T(8,128)} %stack.2), calls=%async_computation | async-start | bytes 67108864 | tf_op jit(solution)/shard_map/all_to_all | solution.py:26
  31.8 0.0 copy-start.1
  31.8 0.0 all-gather.2.cloned.1.call-start
  31.8 0.7 all-gather.2.cloned.1.call-update
  32.5 0.0 copy-done.2
  32.5 0.2 fusion.3
  32.7 52.9 %all-gather.2.cloned.1.call-done = f32[128,8192]{1,0:T(8,128)} async-done(((f32[128,2048]{1,0:T(8,128)}), f32[128,8192]{1,0:T(8,128)}) %all-gather.2.cloned.1.call-update) | async-done | bytes 4194320 | tf_op jit(solution)/shard_map/all_gather | solution.py:8
  85.6 676.1 %all-to-all-done = f32[64,128,1024]{2,1,0:T(8,128)} async-done(((f32[64,128,1024]{2,1,0:T(8,128)}), f32[64,128,1024]{2,1,0:T(8,128)}, u32[]{:S(2)}, u32[]{:S(2)}) %all-to-all-start) | async-done | bytes 33554464 | tf_op jit(solution)/shard_map/all_to_all | solution.py:26
  761.7 0.0 copy-start
  761.7 1.1 broadcast_in_dim.2
  762.8 0.0 copy-done.1
  762.8 1.0 copy-done
  763.8 0.0 copy-start.3
  763.8 25.7 %multiply_reduce_fusion = (f32[1024]{0:T(1024)S(1)}, f32[128,1024]{1,0:T(8,128)}) fusion(f32[128,1024]{1,0:T(8,128)S(1)} %copy-done.1, f32[8192,1024]{1,0:T(8,128)} %bitcast, f32[128,8192]{1,0:T(8,128)S(1)} %copy-done, f32[16,8,64,128]{3,2,1,0:T(8,128)S(1)} %bitcast.10), kind=kOutput, calls=%fused_computation.4 | convolution fusion | flops 12886342656 | bytes 42995712 | tf_op jit(solution)/shard_map/dot_general | solution.py:23
  789.6 135.4 %psum.7 = f32[1024]{0:T(1024)S(1)} all-reduce(f32[1024]{0:T(1024)S(1)} %get-tuple-element.2), channel_id=1, replica_groups=mesh['row'=64,'col'=4] {'row'}, use_global_device_ids=true, to_apply=%region_1.2 | all-reduce | flops 1024 | bytes 8192 | tf_op jit(solution)/shard_map/psum | solution.py:33
  925.0 0.0 copy-done.3
  925.0 0.6 sub.10
  (1 shorter events, 0.0 us)
Async XLA Ops:
  19.2 13.3 %copy-start.2 = (s32[64,64]{1,0:T(8,128)S(1)}, s32[64,64]{1,0:T(8,128)}, u32[]{:S(2)}) copy-start(s32[64,64]{1,0:T(8,128)} %param.6) | copy-start | bytes 49156
  19.3 742.4 %all-to-all-start = ((f32[64,128,1024]{2,1,0:T(8,128)}), f32[64,128,1024]{2,1,0:T(8,128)}, u32[]{:S(2)}, u32[]{:S(2)}) async-start(f32[64,128,1024]{2,1,0:T(8,128)} %stack.2), calls=%async_computation | async-start | bytes 67108864 | tf_op jit(solution)/shard_map/all_to_all | solution.py:26
  31.8 731.0 %copy-start.1 = (f32[128,1024]{1,0:T(8,128)S(1)}, f32[128,1024]{1,0:T(8,128)}, u32[]{:S(2)}) copy-start(f32[128,1024]{1,0:T(8,128)} %param.5) | copy-start | bytes 1572868
  31.8 53.8 %all-gather.2.cloned.1.call-start = ((), (), s32[]{:S(2)}) async-start(), calls=%async_computation.1 | async-start | bytes 5242880 | tf_op jit(solution)/shard_map/all_gather | solution.py:8
  761.7 2.2 copy-start
  763.8 161.1 %copy-start.3 = (f32[1024]{0:T(1024)S(1)}, f32[1024]{0:T(1024)}, u32[]{:S(2)}) copy-start(f32[1024]{0:T(1024)} %param.7) | copy-start | bytes 12292
Sparse Core Ops, SparseCore 0:
  34.4 51.1 all-gather.1

commit v2 on v0

--- a/solution.py
+++ b/solution.py
@@ -28,7 +28,8 @@
     )
     sigma_cross = -product
     partial_value = jnp.sum(panel_hat * sigma_cross, axis=0)
-    summed = lax.psum(partial_value, "row")
+    masks_return_all = lambda target: jnp.sum(lax.all_gather(target, "row"), axis=0)
+    summed = masks_return_all(partial_value)
     variance = diag_inverse - summed
     return (sigma_cross, variance)
 

time: 369 us -> 288 us (0.78)
  blocking collectives: 126 us -> 42.3 us
    psum x1 -> x0, blocking collectives: 126 us -> none  [body(): summed = lax.psum(partial_value, 'row')]
    all_gather x0 -> x1, blocking collectives: none -> 42.3 us  [body(): lax.all_gather(target, 'row')]
where the time goes in v2:
time: 288 us; the launch traced here: 286 us
  waiting for transfers between devices  200 us (69%)
  blocking collectives  42.3 us (15%)
  matrix products  26.7 us (9%)
  between operations  14.1 us (5%)
    all_gather x1, waiting for transfers between devices, body(): lax.all_gather(panel_hat, 'row', axis=0, tiled=True)  145 us
    all_gather x1, waiting for transfers between devices, body(): sigma_rows = lax.all_gather(sigma_anc, 'col', axis=1, tiled=True)  53.2 us
    all_gather x1, blocking collectives, body(): lax.all_gather(target, 'row')  42.3 us
    dot_general x1, matrix products, body(): jnp.dot(masked, lax.all_gather(panel_hat, 'row', axis=0, tiled=True), pre...  25.7 us
  transfers between devices with their start and end apart: 2, of which 2 were waited for; matrix products, arithmetic and copies ran while one was open for 0% of the time, Pallas kernels for 0%

profile of v2, /device:TPU:2, one launch (start us, length us, event | category | flops | bytes accessed | tf_op | source)
XLA Modules:
  0.0 286.1 jit_solution(8327741578123679377)
XLA Ops:
  7.2 0.0 copy-start.1
  7.2 0.0 all-gather.4.cloned.1.call-start
  7.2 0.7 all-gather.4.cloned.1.call-update
  7.9 0.0 all-gather.6.cloned.1.call-start
  8.0 0.7 all-gather.6.cloned.1.call-update
  8.7 1.0 fusion.3
  9.6 53.2 %all-gather.4.cloned.1.call-done = f32[128,8192]{1,0:T(8,128)} async-done(((f32[128,2048]{1,0:T(8,128)}), f32[128,8192]{1,0:T(8,128)}) %all-gather.4.cloned.1.call-update) | async-done | bytes 4194320 | tf_op jit(solution)/shard_map/all_gather | solution.py:8
  62.9 145.4 %all-gather.6.cloned.1.call-done = f32[8192,1024]{1,0:T(8,128)} async-done(((f32[128,1024]{1,0:T(8,128)}), f32[8192,1024]{1,0:T(8,128)}) %all-gather.6.cloned.1.call-update) | async-done | bytes 33554448 | tf_op jit(solution)/shard_map/all_gather | solution.py:25
  208.3 0.0 copy-start
  208.3 1.1 broadcast_in_dim.2
  209.4 0.0 copy-done.1
  209.5 1.0 copy-done
  210.5 0.0 copy-start.2
  210.5 25.7 %multiply_reduce_fusion = (f32[1024]{0:T(1024)S(1)}, f32[128,1024]{1,0:T(8,128)}) fusion(f32[128,1024]{1,0:T(8,128)S(1)} %copy-done.1, f32[8192,1024]{1,0:T(8,128)} %all-gather.6.cloned.1.call-done, f32[128,8192]{1,0:T(8,128)S(1)} %copy-done, f32[16,8,64,128]{3,2,1,0:T(8,128)S(1)} %bitcast.9), kind=kOutput, calls=%fused_computation.4 | convolution fusion | flops 12886342656 | bytes 42995712 | tf_op jit(solution)/shard_map/dot_general | solution.py:23
  236.2 42.3 %all-gather = f32[65536]{0:T(1024)S(1)} all-gather(f32[1024]{0:T(1024)S(1)} %get-tuple-element.2), channel_id=2, replica_groups=mesh['row'=64,'col'=4] {'row'}, dimensions={0}, use_global_device_ids=true | all-gather | bytes 266240 | tf_op jit(solution)/shard_map/all_gather | solution.py:31
  278.6 0.0 copy-done.2
  278.6 0.6 sub.10
  (3 shorter events, 0.1 us)
Async XLA Ops:
  7.2 202.3 %copy-start.1 = (f32[128,1024]{1,0:T(8,128)S(1)}, f32[128,1024]{1,0:T(8,128)}, u32[]{:S(2)}) copy-start(f32[128,1024]{1,0:T(8,128)} %param.5) | copy-start | bytes 1572868
  7.2 55.7 %all-gather.4.cloned.1.call-start = ((), (), s32[]{:S(2)}) async-start(), calls=%async_computation | async-start | bytes 5242880 | tf_op jit(solution)/shard_map/all_gather | solution.py:8
  7.9 200.4 %all-gather.6.cloned.1.call-start = ((), (), s32[]{:S(2)}) async-start(), calls=%async_computation.1 | async-start | bytes 34078720 | tf_op jit(solution)/shard_map/all_gather | solution.py:25
  208.3 2.2 copy-start
  210.5 68.1 %copy-start.2 = (f32[1024]{0:T(1024)S(1)}, f32[1024]{0:T(1024)}, u32[]{:S(2)}) copy-start(f32[1024]{0:T(1024)} %param.7) | copy-start | bytes 12292
Sparse Core Ops, SparseCore 0:
  9.8 53.0 all-gather.3
  65.6 142.6 all-gather.5
